TPU v7x, 32 devices: a whole 2x2x4 slice. The times are simulated.
32 devices in a mesh: lat: 8 (over y, x, core), grp: 4 (over z).
Axes of the slice: x: 2, y: 2, z: 4, core: 2. Of those that a mesh axis runs over, the one named last changes fastest.
Arguments:
- increments: bfloat16 [2048, 4, 16, 128], P(('lat', 'grp')), may hold values from -6 to 6
- band: int32 [2048, 1], P(('lat', 'grp')), may hold values from 0 to 7; in each aligned block of 64 rows (0 to 63, 64 to 127, ...) at most 24 rows name the same one
- tile_index: int32 [2048], P(('lat', 'grp')), may hold values from 0 to 7
- lat_offset: int32 [2048], P(('lat', 'grp')), may hold values from 0 to 12
- lon_shift: int32 [2048], P(('lat', 'grp')), may hold values from -8 to 8
- lat_frac: float32 [2048], P(('lat', 'grp')), may hold values from 0 to 1
- lon_frac: float32 [2048, 128], P(('lat', 'grp')), may hold values from 0 to 1
Outputs:
- source_adjoint: float32 [16, 4, 1024, 128], P('grp', None, 'lat')
Inputs may be any that keep to these rules, and one draw needn't show every extreme that they name: In the rows of one device no band is named more than 24 times, a bound that some block reaches.
All inputs are finite; a program needn't handle non-finite values.
Results may differ from a plain program's by a relative error of at most 0.0045.
Values may be sent and summed in bfloat16 or wider, within the bound.
A program may use at most 64 MiB of HBM per device.

v0:
```python
import functools
import math

import jax
import jax.numpy as jnp
from jax import lax
from jax.experimental import pallas as pl
from jax.experimental.pallas import tpu as pltpu
from jax.sharding import PartitionSpec as P

TL = 16
TILES_DEV = 8


def lagrange(fraction):
    return [
        -fraction * (fraction - 1.0) * (fraction - 2.0) / 6.0,
        (fraction + 1.0) * (fraction - 1.0) * (fraction - 2.0) / 2.0,
        -(fraction + 1.0) * fraction * (fraction - 2.0) / 2.0,
        (fraction + 1.0) * fraction * (fraction - 1.0) / 6.0,
    ]


def lon_adjoint(increments, lon_shift, lon_frac):
    row_count, fields, levels, points = increments.shape
    lon_weight = [w.astype(jnp.bfloat16) for w in lagrange(lon_frac)]
    source = jnp.arange(points, dtype=jnp.int32)[None, :, None]
    target = jnp.arange(points, dtype=jnp.int32)[None, None, :]
    width = math.gcd(row_count, 32)
    nothing = jnp.zeros((), jnp.bfloat16)

    def one_block(number):
        first = number * width
        shifts = lax.dynamic_slice_in_dim(lon_shift, first, width, 0)
        own_matrix = jnp.zeros((width, points, points), jnp.bfloat16)
        spill_matrix = jnp.zeros((width, points, points), jnp.bfloat16)
        for m in range(4):
            weight = lax.dynamic_slice_in_dim(lon_weight[m], first, width, 0)[:, :, None]
            landing = source + shifts[:, None, None] + m - 1
            own_matrix = own_matrix + jnp.where(target == landing, weight, nothing)
            wrapped = (target == landing - points) | (target == landing + points)
            spill_matrix = spill_matrix + jnp.where(wrapped, weight, nothing)
        values = lax.dynamic_slice_in_dim(increments, first, width, 0)
        own = jnp.einsum(
            "bflj,bjc->bflc", values, own_matrix, preferred_element_type=jnp.float32
        ).astype(jnp.bfloat16)
        spill = jnp.einsum(
            "bflj,bjc->bflc", values, spill_matrix, preferred_element_type=jnp.float32
        ).astype(jnp.bfloat16)
        return (own, spill)

    own, spill = lax.map(one_block, jnp.arange(row_count // width, dtype=jnp.int32))
    return (
        own.reshape(row_count, fields, levels, points),
        spill.reshape(row_count, fields, levels, points),
    )


def tile_terms(columns, own_rows, spill_rows):
    points = own_rows.shape[3]
    low_half = (jnp.arange(points, dtype=jnp.int32) < points // 2)[None, None, None, :]
    nothing = jnp.zeros((), jnp.bfloat16)
    spill_next = jnp.where(low_half, spill_rows, nothing)
    spill_prev = jnp.where(low_half, nothing, spill_rows)
    result = jnp.einsum("sq,sflc->lfqc", columns[0], own_rows, preferred_element_type=jnp.float32)
    result = result + jnp.einsum(
        "sq,sflc->lfqc", columns[1], spill_next, preferred_element_type=jnp.float32
    )
    return result + jnp.einsum(
        "sq,sflc->lfqc", columns[2], spill_prev, preferred_element_type=jnp.float32
    )


def by_slots(increments, band, tile_index, lat_offset, lon_shift, lat_frac, lon_frac):
    row_count, fields, levels, points = increments.shape
    n_lat = lax.axis_size("lat")
    capacity = 3 * row_count // n_lat
    tile_rows = TILES_DEV * TL
    own, spill = lon_adjoint(increments, lon_shift, lon_frac)
    lat_weight = [w.astype(jnp.bfloat16) for w in lagrange(lat_frac)]
    tile_slots = jnp.arange(tile_rows, dtype=jnp.int32)[None, :]
    nothing = jnp.zeros((), jnp.bfloat16)

    def stencil_columns(tile_number):
        base_row = tile_number * TL + lat_offset
        table = jnp.zeros((row_count, tile_rows), jnp.bfloat16)
        for k in range(4):
            table = table + jnp.where(
                tile_slots == base_row[:, None] + k, lat_weight[k][:, None], nothing
            )
        return table

    here_columns = stencil_columns(tile_index)
    next_columns = stencil_columns((tile_index + 1) % TILES_DEV)
    prev_columns = stencil_columns((tile_index + TILES_DEV - 1) % TILES_DEV)
    destination = band[:, 0]
    one_hot = (destination[:, None] == jnp.arange(n_lat, dtype=jnp.int32)[None, :]).astype(
        jnp.int32
    )
    position = jnp.sum(jnp.cumsum(one_hot, axis=0) * one_hot, axis=1) - 1
    slot_index = destination * capacity + position

    def to_slots(values):
        empty = jnp.zeros((n_lat * capacity,) + values.shape[1:], jnp.bfloat16)
        placed = empty.at[slot_index].set(values)
        return placed.reshape((n_lat, capacity) + values.shape[1:])

    send_own = to_slots(own)
    send_spill = to_slots(spill)
    send_here = to_slots(here_columns)
    send_next = to_slots(next_columns)
    send_prev = to_slots(prev_columns)
    got = (
        lax.all_to_all(send_own, "lat", split_axis=0, concat_axis=0, tiled=True),
        lax.all_to_all(send_spill, "lat", split_axis=0, concat_axis=0, tiled=True),
        lax.all_to_all(send_here, "lat", split_axis=0, concat_axis=0, tiled=True),
        lax.all_to_all(send_next, "lat", split_axis=0, concat_axis=0, tiled=True),
        lax.all_to_all(send_prev, "lat", split_axis=0, concat_axis=0, tiled=True),
    )
    flat_own = got[0].reshape(-1, fields, levels, points)
    flat_spill = got[1].reshape(-1, fields, levels, points)
    flat_columns = (
        got[2].reshape(-1, tile_rows),
        got[3].reshape(-1, tile_rows),
        got[4].reshape(-1, tile_rows),
    )
    return lax.psum_scatter(
        tile_terms(flat_columns, flat_own, flat_spill), "grp", scatter_dimension=0, tiled=True
    )


MESH = pl.DeviceIdType.MESH


def fused_kernel(n_lat, n_grp, per, x_ref, frac_ref, band_ref, tile_ref, first_ref, shift_ref, part_ref, out_ref, meta_ref, xs, fr, mt, wl, am, rb, pb, s1, r1, s2, r2,
                 z_send, z_recv, f_send, f_recv, m_send, m_recv, c_send, c_recv, n_send, n_recv,
                 d_send, d_recv, e_send, e_recv, loc_sem):
    lat = lax.axis_index("lat")
    grp = lax.axis_index("grp")
    chip, core = lat // 2, lat % 2
    mate = chip * 2 + (1 - core)
    n_chip = n_lat // 2
    units, rows, points = xs.shape[1:]
    chunks, half = units // per, per // 2
    tile_rows = am.shape[0] // n_chip
    block = n_grp * rows
    part_rows = 16

    def toggled(bit):
        return chip + bit * (1 - 2 * ((chip // bit) % 2))

    across = (toggled(1), toggled(2))
    opposite = toggled(1) + toggled(2) - chip
    chips = (chip, across[0], across[1], opposite)

    meta_ref[...] = jnp.zeros_like(meta_ref)
    meta_ref[0:1, 0:rows] = band_ref[...].astype(jnp.float32)
    meta_ref[1:2, 0:rows] = (tile_ref[...] * TL + first_ref[...]).astype(jnp.float32)
    meta_ref[2:3, 0:rows] = shift_ref[...].astype(jnp.float32)
    meta_ref[3:4, 0:rows] = part_ref[...]

    barrier = pltpu.get_barrier_semaphore()
    for d in range(1, n_grp):
        pl.semaphore_signal(barrier, inc=1, device_id=(lat, (grp + d) % n_grp), device_id_type=MESH)
    pl.semaphore_signal(barrier, inc=1, device_id=(mate, grp), device_id_type=MESH)
    for to in across:
        pl.semaphore_signal(barrier, inc=1, device_id=(to * 2 + core, grp), device_id_type=MESH)
    pl.semaphore_wait(barrier, n_grp + 2)

    def remote(src, dst, send, recv, to):
        return pltpu.make_async_remote_copy(
            src_ref=src, dst_ref=dst, send_sem=send, recv_sem=recv, device_id=to, device_id_type=MESH
        )

    def source(d):
        bits = [1 << n for n in range(n_grp.bit_length()) if d & (1 << n)]
        return grp + sum(bit * (1 - 2 * ((grp // bit) % 2)) for bit in bits)

    def f_copy(d, g):
        return remote(frac_ref, fr.at[g], f_send.at[d], f_recv.at[g], (lat, source(d)))

    def m_copy(d, g):
        return remote(meta_ref, mt.at[core, g], m_send.at[d], m_recv.at[g], (lat, source(d)))

    def n_copy(d):
        g = source(d)
        src = meta_ref if d == 0 else mt.at[core, g]
        return remote(src, mt.at[core, g], n_send.at[d], n_recv.at[g], (mate, grp))

    def z_copy(d, v, g):
        to = source(d)
        return remote(x_ref.at[pl.ds(to * units + v * per, per)], xs.at[g, pl.ds(v * per, per)],
                      z_send.at[d, v], z_recv.at[g, v], (lat, to))

    def c_copy(v):
        mine = rb.at[pl.ds(v * per, per), pl.ds(core * block, block)]
        return remote(mine, mine, c_send.at[v], c_recv.at[v], (mate, grp))

    def d_copy(v, a):
        return remote(s1.at[v, a], r1.at[v, a], d_send.at[v, a], d_recv.at[v, a], (across[a] * 2 + core, grp))

    def e_copy(v, a):
        return remote(s2.at[v, a], r2.at[v, a], e_send.at[v, a], e_recv.at[v, a], (across[1 - a] * 2 + core, grp))

    own_x = pltpu.make_async_copy(x_ref.at[pl.ds(grp * units, units)], xs.at[grp], loc_sem.at[0])
    own_f = pltpu.make_async_copy(frac_ref, fr.at[grp], loc_sem.at[1])
    own_m = pltpu.make_async_copy(meta_ref, mt.at[core, grp], loc_sem.at[2])
    own_f.start()
    own_m.start()
    for d in range(1, n_grp):
        m_copy(d, grp).start()
    for d in range(1, n_grp):
        f_copy(d, grp).start()
    n_copy(0).start()
    for v in range(chunks):
        for near in range(2 * v, min(2 * v + 2, chunks)):
            z_copy(1, near, grp).start()
        for d in range(2, n_grp):
            z_copy(d, v, grp).start()
    own_x.start()

    lane = lax.broadcasted_iota(jnp.int32, (rows, points), 1)
    eye = lax.broadcasted_iota(jnp.int32, (rows, points), 0) == lane
    steps = (1, 2, 4, 8, 16)

    def turn(values, amount):
        return pltpu.roll(values, amount % points, 1)

    def weights_of(g):
        shift_lanes = mt[core, g, 2:3, :]
        diagonal = jnp.where(eye, shift_lanes, 0.0).astype(jnp.bfloat16)
        shift = jnp.dot(
            diagonal, jnp.ones((points, points), jnp.bfloat16), preferred_element_type=jnp.float32
        ).astype(jnp.int32)
        bits = shift + 8
        fraction = (fr[g].astype(jnp.int32).astype(jnp.float32) + 32768.0) * (1.0 / 65535.0)
        for m, weight in enumerate(lagrange(fraction)):
            weight = weight.astype(jnp.bfloat16).astype(jnp.float32)
            for step in steps:
                weight = jnp.where((bits & step) != 0, turn(weight, step), weight)
            weight = turn(weight, m - 9)
            raw = lane - shift - (m - 1)
            inside = (raw >= 0) & (raw < points)
            wl[g, m] = jnp.where(inside, weight, 0.0)
            wl[g, 4 + m] = jnp.where(inside, 0.0, weight)
        wl[g, 8] = bits.astype(jnp.float32)

    own_f.wait()
    own_m.wait()
    weights_of(grp)
    for d in range(1, n_grp):
        m_copy(d, source(d)).wait_recv()
        n_copy(d).start()
    for d in range(1, n_grp):
        f_copy(d, source(d)).wait_recv()
        weights_of(source(d))

    wide = lax.broadcasted_iota(jnp.int32, (8, 2 * rows), 1)
    slot = lax.broadcasted_iota(jnp.int32, (tile_rows, 2 * rows), 0)

    def table_of(c, g):
        both = jnp.where(wide < rows, mt[c, g], pltpu.roll(mt[c, g + 1], rows, 1))
        band = both[0:1].astype(jnp.int32)
        place = both[1:2].astype(jnp.int32)
        lat_weight = [w.astype(jnp.bfloat16).astype(jnp.float32) for w in lagrange(both[3:4])]
        for e in range(n_chip):
            far = slot - jnp.where(band == chips[e] * 2 + core, place, -(1 << 20))
            table = jnp.zeros(far.shape, jnp.float32)
            for k in range(4):
                table = jnp.where(far == k, lat_weight[k], table)
            am[pl.ds(e * tile_rows, tile_rows), pl.ds(c * block + g * rows, 2 * rows)] = table.astype(jnp.bfloat16)

    for d in range(n_grp):
        g = source(d)
        remote(meta_ref, mt.at[1 - core, g], n_send.at[d], n_recv.at[g], (mate, grp)).wait_recv()
    for c in range(2):
        for g in range(0, n_grp, 2):
            table_of(c, g)
    own_x.wait()

    def lon(g, v):
        bits = wl[g, 8].astype(jnp.int32)
        place = pl.ds(core * block + g * rows, rows)
        moved = [xs[g, v * per + f].astype(jnp.float32) for f in range(per)]
        for step in steps:
            mask = (bits & step) != 0
            moved = [jnp.where(mask, turn(x, step), x) for x in moved]
        own, spill = [0.0] * per, [0.0] * per
        for m in range(4):
            here, gone = wl[g, m], wl[g, 4 + m]
            for f in range(per):
                x = turn(moved[f], m - 9)
                own[f] = own[f] + x * here
                spill[f] = spill[f] + x * gone
        for f in range(per):
            rb[v * per + f, place, 0:points] = own[f].astype(jnp.bfloat16)
            rb[v * per + f, place, points:2 * points] = spill[f].astype(jnp.bfloat16)

    low = lax.broadcasted_iota(jnp.int32, (tile_rows, points), 1) < points // 2

    def arrive(v):
        for d in range(1, n_grp):
            z_copy(d, v, source(d)).wait_recv()

        def one(g, carry):
            lon(g, v)
            return carry

        lax.fori_loop(0, n_grp, one, 0, unroll=True)
        c_copy(v).start()

    def depart(v):
        theirs = rb.at[pl.ds(v * per, per), pl.ds((1 - core) * block, block)]
        remote(theirs, theirs, c_send.at[v], c_recv.at[v], (mate, grp)).wait_recv()
        for f in range(per):
            a, at = f // half, f % half
            whole = jnp.dot(am[...], rb[v * per + f], preferred_element_type=jnp.float32)
            for e in range(n_chip):
                both = whole[e * tile_rows:(e + 1) * tile_rows]
                own, spill = both[:, :points], both[:, points:]
                ahead = jnp.concatenate([spill[-TL:], spill[:-TL]], axis=0)
                behind = jnp.concatenate([spill[TL:], spill[:TL]], axis=0)
                total = own + jnp.where(low, ahead, behind)
                if e == 0:
                    out_ref[v * per + f] = total
                elif e == 3:
                    s1[v, a, 1, at] = total.astype(jnp.bfloat16)
                elif e == a + 1:
                    s1[v, a, 0, at] = total.astype(jnp.bfloat16)
                else:
                    pb[v % 4, f] = total
            if at == half - 1:
                d_copy(v, a).start()

    def middle(v):
        for a in range(2):
            d_copy(v, a).wait_recv()
            for at in range(half):
                total = pb[v % 4, a * half + at] + r1[v, a, 1, at].astype(jnp.float32)
                s2[v, a, at] = total.astype(jnp.bfloat16)
            e_copy(v, a).start()

    def finish(v):
        for a in range(2):
            e_copy(v, a).wait_recv()
            for at in range(half):
                unit = v * per + a * half + at
                out_ref[unit] = out_ref[unit] + r1[v, a, 0, at].astype(jnp.float32) + r2[v, a, at].astype(jnp.float32)

    def chunk(v, carry):
        @pl.when(v < chunks)
        def _():
            arrive(v)

        @pl.when((v >= 1) & (v < chunks + 1))
        def _():
            depart(v - 1)

        @pl.when((v >= 3) & (v < chunks + 3))
        def _():
            middle(v - 3)

        @pl.when(v >= 5)
        def _():
            finish(v - 5)

        return carry

    lax.fori_loop(0, chunks + 5, chunk, 0)

    n_copy(0).wait_send()
    for d in range(1, n_grp):
        f_copy(d, grp).wait_send()
        m_copy(d, grp).wait_send()
        n_copy(d).wait_send()
    for v in range(chunks):
        for d in range(1, n_grp):
            z_copy(d, v, grp).wait_send()
        c_copy(v).wait_send()
        for a in range(2):
            d_copy(v, a).wait_send()
            e_copy(v, a).wait_send()


def fused(increments, band, tile_index, lat_offset, lon_shift, lat_frac, lon_frac):
    rows, fields, all_levels, points = increments.shape
    n_lat, n_grp = lax.axis_size("lat"), lax.axis_size("grp")
    n_chip = n_lat // 2
    levels = all_levels // n_grp
    tile_rows = TILES_DEV * TL
    units = levels * fields
    per = 2
    chunks = units // per
    x = jnp.transpose(increments, (2, 1, 0, 3)).reshape(all_levels * fields, rows, points)
    small = [a.reshape(1, rows) for a in (band, tile_index, lat_offset, lon_shift, lat_frac)]
    coded = (jnp.round(lon_frac * 65535.0) - 32768.0).astype(jnp.int16)
    bf16, f32 = jnp.bfloat16, jnp.float32
    dma = pltpu.SemaphoreType.DMA
    return pl.pallas_call(
        functools.partial(fused_kernel, n_lat, n_grp, per),
        out_shape=jax.ShapeDtypeStruct((units, tile_rows, points), f32),
        in_specs=[pl.BlockSpec(memory_space=pltpu.VMEM)] * 7,
        out_specs=pl.BlockSpec(memory_space=pltpu.VMEM),
        scratch_shapes=[
            pltpu.VMEM((8, points), f32),
            pltpu.VMEM((n_grp, units, rows, points), bf16),
            pltpu.VMEM((n_grp, rows, points), jnp.int16),
            pltpu.VMEM((2, n_grp, 8, points), f32),
            pltpu.VMEM((n_grp, 9, rows, points), f32),
            pltpu.VMEM((n_chip * tile_rows, n_grp * 2 * rows), bf16),
            pltpu.VMEM((units, n_grp * 2 * rows, 2 * points), bf16),
            pltpu.VMEM((4, per, tile_rows, points), f32),
            pltpu.VMEM((chunks, 2, 2, per // 2, tile_rows, points), bf16),
            pltpu.VMEM((chunks, 2, 2, per // 2, tile_rows, points), bf16),
            pltpu.VMEM((chunks, 2, per // 2, tile_rows, points), bf16),
            pltpu.VMEM((chunks, 2, per // 2, tile_rows, points), bf16),
            dma((n_grp, chunks)),
            dma((n_grp, chunks)),
            dma((n_grp,)),
            dma((n_grp,)),
            dma((n_grp,)),
            dma((n_grp,)),
            dma((chunks,)),
            dma((chunks,)),
            dma((n_grp,)),
            dma((n_grp,)),
            dma((chunks, 2)),
            dma((chunks, 2)),
            dma((chunks, 2)),
            dma((chunks, 2)),
            dma((3,)),
        ],
        compiler_params=pltpu.CompilerParams(
            collective_id=0, has_side_effects=True, vmem_limit_bytes=40 * 1024 * 1024
        ),
    )(x, coded, *small).reshape(levels, fields, tile_rows, points)


def solution(mesh):
    in_specs = (
        P(("lat", "grp"), None, None, None),
        P(("lat", "grp"), None),
        P(("lat", "grp")),
        P(("lat", "grp")),
        P(("lat", "grp")),
        P(("lat", "grp")),
        P(("lat", "grp"), None),
    )
    out_specs = P("grp", None, "lat", None)
    n_lat, n_grp = mesh.shape["lat"], mesh.shape["grp"]

    def local(increments, *rest):
        rows = increments.shape[0]
        dense_rows = n_lat // 2 * TILES_DEV * TL
        slot_rows = n_grp * n_lat * (3 * rows // n_lat)
        grid = n_lat == 8 and n_grp > 1 and n_grp & (n_grp - 1) == 0
        step = fused if grid and dense_rows <= slot_rows else by_slots
        return step(increments, *rest)

    return jax.shard_map(local, mesh=mesh, in_specs=in_specs, out_specs=out_specs, check_vma=False)
```

profile of v0, /device:TPU:0, one launch (start us, length us, event | category | flops | bytes accessed | tf_op | source)
XLA Modules:
  0.0 50.0 jit_solution(8076062023550196735)
XLA Ops:
  0.0 0.8 %add_convert_fusion.frac_ref = s16[64,128]{1,0:T(8,128)(2,1)S(1)} fusion(f32[64,128]{1,0:T(8,128)} %param.13), kind=kLoop, calls=%fused_computation | loop fusion | flops 32768 | bytes 49152 | tf_op jit(solution)/shard_map/convert_element_type | solution.py:396
  0.8 0.0 copy-start.3
  0.8 0.0 copy-start.4
  0.8 1.9 %copy.8 = bf16[16,4,64,128]{3,2,1,0:T(8,128)(2,1)S(1)} copy(bf16[16,4,64,128]{3,0,1,2:T(8,128)(2,1)} %bitcast.15) | data formatting | bytes 2097152 | tf_op jit(solution)/shard_map/transpose | solution.py:394
  2.7 0.0 copy-start
  2.7 0.0 copy-start.1
  2.7 0.0 copy-start.2
  2.7 0.0 copy-done.3
  2.8 0.0 copy-done.4
  2.8 0.6 %copy-done = s32[64,1]{0,1:T(1,128)S(1)} copy-done((s32[64,1]{0,1:T(1,128)S(1)}, s32[64,1]{0,1:T(1,128)}, u32[]{:S(2)}) %copy-start) | copy-done | bytes 280
  3.4 0.0 copy-done.1
  3.4 0.0 copy-done.2
  3.4 45.6 %shard_map.73 = f32[16,128,128]{2,1,0:T(8,128)S(1)} custom-call(bf16[64,64,128]{2,1,0:T(8,128)(2,1)S(1)} %bitcast.9, s16[64,128]{1,0:T(8,128)(2,1)S(1)} %add_convert_fusion.frac_ref, s32[1,64]{1,0:T(1,128)S(1)} %bitcast.10, s32[1,64]{1,0:T(1,128)S(1)} %bitcast.11, s32[1,64]{1,0:T(1,128)S(1)} %bitcast.12, s32[1,64]{1,0:T(1,128)S(1)} %bitcast.13, ...), custom_call_target="tpu_custom_call" | custom-call | tf_op jit(solution)/shard_map/pallas_call | solution.py:399
  49.0 1.0 %copy.10 = f32[4,4,128,128]{3,2,1,0:T(8,128)} copy(f32[4,4,128,128]{3,2,1,0:T(8,128)S(1)} %bitcast.8) | data formatting | bytes 2097152
Async XLA Ops:
  0.8 2.0 %copy-start.3 = (s32[64]{0:T(128)S(1)}, s32[64]{0:T(128)}, u32[]{:S(2)}) copy-start(s32[64]{0:T(128)} %param.11) | copy-start | bytes 772
  0.8 2.0 %copy-start.4 = (f32[64]{0:T(128)S(1)}, f32[64]{0:T(128)}, u32[]{:S(2)}) copy-start(f32[64]{0:T(128)} %param.12) | copy-start | bytes 772
  2.7 0.7 %copy-start = (s32[64,1]{0,1:T(1,128)S(1)}, s32[64,1]{0,1:T(1,128)}, u32[]{:S(2)}) copy-start(s32[64,1]{0,1:T(1,128)} %param.8) | copy-start | bytes 772
  2.7 0.7 %copy-start.1 = (s32[64]{0:T(128)S(1)}, s32[64]{0:T(128)}, u32[]{:S(2)}) copy-start(s32[64]{0:T(128)} %param.9) | copy-start | bytes 772
  2.7 0.7 %copy-start.2 = (s32[64]{0:T(128)S(1)}, s32[64]{0:T(128)}, u32[]{:S(2)}) copy-start(s32[64]{0:T(128)} %param.10) | copy-start | bytes 772
where the time goes:
time: 50.2 us; the launch traced here: 50 us
  Pallas kernels  45.6 us (91%)
  local copies, waits for them, and re-layouts  3.54 us (7%)
  other arithmetic  0.77 us (2%)
    pallas_call x1, Pallas kernels, fused(): pl.pallas_call(functools.partial(fused_kernel, n_lat, n_grp, per), out_sh...  45.6 us
    transpose x1, local copies, waits for them, and re-layouts, fused(): jnp.transpose(increments, (2, 1, 0, 3))  1.91 us
    unnamed x11, local copies, waits for them, and re-layouts  1.63 us

commit v1 on v0

v1 whole, which is shorter than its diff:
```python
import functools
import math

import jax
import jax.numpy as jnp
from jax import lax
from jax.experimental import pallas as pl
from jax.experimental.pallas import tpu as pltpu
from jax.sharding import PartitionSpec as P

TL = 16
TILES_DEV = 8


def lagrange(fraction):
    return [
        -fraction * (fraction - 1.0) * (fraction - 2.0) / 6.0,
        (fraction + 1.0) * (fraction - 1.0) * (fraction - 2.0) / 2.0,
        -(fraction + 1.0) * fraction * (fraction - 2.0) / 2.0,
        (fraction + 1.0) * fraction * (fraction - 1.0) / 6.0,
    ]


def lon_adjoint(increments, lon_shift, lon_frac):
    row_count, fields, levels, points = increments.shape
    lon_weight = [w.astype(jnp.bfloat16) for w in lagrange(lon_frac)]
    source = jnp.arange(points, dtype=jnp.int32)[None, :, None]
    target = jnp.arange(points, dtype=jnp.int32)[None, None, :]
    width = math.gcd(row_count, 32)
    nothing = jnp.zeros((), jnp.bfloat16)

    def one_block(number):
        first = number * width
        shifts = lax.dynamic_slice_in_dim(lon_shift, first, width, 0)
        own_matrix = jnp.zeros((width, points, points), jnp.bfloat16)
        spill_matrix = jnp.zeros((width, points, points), jnp.bfloat16)
        for m in range(4):
            weight = lax.dynamic_slice_in_dim(lon_weight[m], first, width, 0)[:, :, None]
            landing = source + shifts[:, None, None] + m - 1
            own_matrix = own_matrix + jnp.where(target == landing, weight, nothing)
            wrapped = (target == landing - points) | (target == landing + points)
            spill_matrix = spill_matrix + jnp.where(wrapped, weight, nothing)
        values = lax.dynamic_slice_in_dim(increments, first, width, 0)
        own = jnp.einsum(
            "bflj,bjc->bflc", values, own_matrix, preferred_element_type=jnp.float32
        ).astype(jnp.bfloat16)
        spill = jnp.einsum(
            "bflj,bjc->bflc", values, spill_matrix, preferred_element_type=jnp.float32
        ).astype(jnp.bfloat16)
        return (own, spill)

    own, spill = lax.map(one_block, jnp.arange(row_count // width, dtype=jnp.int32))
    return (
        own.reshape(row_count, fields, levels, points),
        spill.reshape(row_count, fields, levels, points),
    )


def tile_terms(columns, own_rows, spill_rows):
    points = own_rows.shape[3]
    low_half = (jnp.arange(points, dtype=jnp.int32) < points // 2)[None, None, None, :]
    nothing = jnp.zeros((), jnp.bfloat16)
    spill_next = jnp.where(low_half, spill_rows, nothing)
    spill_prev = jnp.where(low_half, nothing, spill_rows)
    result = jnp.einsum("sq,sflc->lfqc", columns[0], own_rows, preferred_element_type=jnp.float32)
    result = result + jnp.einsum(
        "sq,sflc->lfqc", columns[1], spill_next, preferred_element_type=jnp.float32
    )
    return result + jnp.einsum(
        "sq,sflc->lfqc", columns[2], spill_prev, preferred_element_type=jnp.float32
    )


def by_slots(increments, band, tile_index, lat_offset, lon_shift, lat_frac, lon_frac):
    row_count, fields, levels, points = increments.shape
    n_lat = lax.axis_size("lat")
    capacity = 3 * row_count // n_lat
    tile_rows = TILES_DEV * TL
    own, spill = lon_adjoint(increments, lon_shift, lon_frac)
    lat_weight = [w.astype(jnp.bfloat16) for w in lagrange(lat_frac)]
    tile_slots = jnp.arange(tile_rows, dtype=jnp.int32)[None, :]
    nothing = jnp.zeros((), jnp.bfloat16)

    def stencil_columns(tile_number):
        base_row = tile_number * TL + lat_offset
        table = jnp.zeros((row_count, tile_rows), jnp.bfloat16)
        for k in range(4):
            table = table + jnp.where(
                tile_slots == base_row[:, None] + k, lat_weight[k][:, None], nothing
            )
        return table

    here_columns = stencil_columns(tile_index)
    next_columns = stencil_columns((tile_index + 1) % TILES_DEV)
    prev_columns = stencil_columns((tile_index + TILES_DEV - 1) % TILES_DEV)
    destination = band[:, 0]
    one_hot = (destination[:, None] == jnp.arange(n_lat, dtype=jnp.int32)[None, :]).astype(
        jnp.int32
    )
    position = jnp.sum(jnp.cumsum(one_hot, axis=0) * one_hot, axis=1) - 1
    slot_index = destination * capacity + position

    def to_slots(values):
        empty = jnp.zeros((n_lat * capacity,) + values.shape[1:], jnp.bfloat16)
        placed = empty.at[slot_index].set(values)
        return placed.reshape((n_lat, capacity) + values.shape[1:])

    send_own = to_slots(own)
    send_spill = to_slots(spill)
    send_here = to_slots(here_columns)
    send_next = to_slots(next_columns)
    send_prev = to_slots(prev_columns)
    got = (
        lax.all_to_all(send_own, "lat", split_axis=0, concat_axis=0, tiled=True),
        lax.all_to_all(send_spill, "lat", split_axis=0, concat_axis=0, tiled=True),
        lax.all_to_all(send_here, "lat", split_axis=0, concat_axis=0, tiled=True),
        lax.all_to_all(send_next, "lat", split_axis=0, concat_axis=0, tiled=True),
        lax.all_to_all(send_prev, "lat", split_axis=0, concat_axis=0, tiled=True),
    )
    flat_own = got[0].reshape(-1, fields, levels, points)
    flat_spill = got[1].reshape(-1, fields, levels, points)
    flat_columns = (
        got[2].reshape(-1, tile_rows),
        got[3].reshape(-1, tile_rows),
        got[4].reshape(-1, tile_rows),
    )
    return lax.psum_scatter(
        tile_terms(flat_columns, flat_own, flat_spill), "grp", scatter_dimension=0, tiled=True
    )


MESH = pl.DeviceIdType.MESH


def fused_kernel(n_lat, n_grp, x_ref, frac_ref, band_ref, tile_ref, first_ref, shift_ref, part_ref, out_ref,
                 meta_ref, fs, xs, fr, wl, am, rb, pb, s1, r1, q1, s2, q2, s3, r3,
                 z_send, z_recv, f_send, f_recv, n_send, n_recv, x_send, x_recv,
                 d_send, d_recv, p_send, p_recv, e_send, e_recv, o_send, o_recv, loc_sem):
    lat = lax.axis_index("lat")
    grp = lax.axis_index("grp")
    chip, core = lat // 2, lat % 2
    other = 1 - core
    mate = chip * 2 + other
    n_chip = n_lat // 2
    units, rows, points = xs.shape[1:]
    tile_rows = TILES_DEV * TL

    def toggled(bit):
        return chip + bit * (1 - 2 * ((chip // bit) % 2))

    across = (toggled(1), toggled(2))
    opposite = toggled(1) + toggled(2) - chip
    parity = (core, other)
    first = tuple(across[0] * (1 - q) + across[1] * q for q in parity)
    second = tuple(across[1] * (1 - q) + across[0] * q for q in parity)

    def source(d):
        bits = [1 << n for n in range(n_grp.bit_length()) if d & (1 << n)]
        return grp + sum(bit * (1 - 2 * ((grp // bit) % 2)) for bit in bits)

    barrier = pltpu.get_barrier_semaphore()
    for d in range(1, n_grp):
        for q in parity:
            pl.semaphore_signal(barrier, inc=1, device_id=(chip * 2 + q, source(d)), device_id_type=MESH)
    pl.semaphore_signal(barrier, inc=1, device_id=(mate, grp), device_id_type=MESH)
    for to in across:
        for q in parity:
            pl.semaphore_signal(barrier, inc=1, device_id=(to * 2 + q, grp), device_id_type=MESH)

    def coded(fraction):
        return jnp.round(fraction * 65535.0) - 32768.0

    def decoded(code):
        return (code.astype(jnp.float32) + 32768.0) * (1.0 / 65535.0)

    meta_ref[...] = jnp.zeros_like(meta_ref)
    meta_ref[0:1, 0:rows] = band_ref[...].astype(jnp.float32)
    meta_ref[1:2, 0:rows] = (tile_ref[...] * TL + first_ref[...]).astype(jnp.float32)
    meta_ref[2:3, 0:rows] = shift_ref[...].astype(jnp.float32)
    meta_ref[3:4, 0:rows] = coded(part_ref[...])
    fs[0:rows] = coded(frac_ref[...]).astype(jnp.int32).astype(jnp.int16)
    fs[rows:rows + 8] = meta_ref[...].astype(jnp.int32).astype(jnp.int16)

    pl.semaphore_wait(barrier, 2 * (n_grp - 1) + 1 + 4)

    def remote(src, dst, send, recv, to):
        return pltpu.make_async_remote_copy(
            src_ref=src, dst_ref=dst, send_sem=send, recv_sem=recv, device_id=to, device_id_type=MESH
        )

    def f_copy(d, g):
        return remote(fs, fr.at[g], f_send.at[d], f_recv.at[g], (lat, source(d)))

    def n_copy(d):
        g = source(d)
        src = fs if d == 0 else fr.at[g]
        return remote(src, fr.at[n_grp + g], n_send.at[d], n_recv.at[g], (mate, grp))

    def z_copy(d, v, j, g):
        to, q = source(d), parity[j]
        return remote(x_ref.at[(to * 2 + q) * units + v], xs.at[j * n_grp + g, v],
                      z_send.at[d, j, v], z_recv.at[g, j, v], (chip * 2 + q, to))

    def x_copy():
        return remote(x_ref.at[pl.ds((grp * 2 + other) * units, units)], xs.at[n_grp + grp],
                      x_send, x_recv, (mate, grp))

    def d_copy(v, j):
        return remote(s1.at[v, j, 0], q1.at[v, j], d_send.at[v, j], d_recv.at[v, j], (first[j] * 2 + parity[j], grp))

    def p_copy(v, j):
        return remote(s1.at[v, j, 1], r1.at[v, j], p_send.at[v, j], p_recv.at[v, j], (first[j] * 2 + core, grp))

    def e_copy(v, j):
        return remote(s2.at[v, j], q2.at[v, j], e_send.at[v, j], e_recv.at[v, j], (second[j] * 2 + parity[j], grp))

    def o_copy(v):
        return remote(s3.at[v], r3.at[v], o_send.at[v], o_recv.at[v], (mate, grp))

    own_x = pltpu.make_async_copy(x_ref.at[pl.ds((grp * 2 + core) * units, units)], xs.at[grp], loc_sem)
    for d in range(1, n_grp):
        f_copy(n_grp - d, grp).start()
    n_copy(0).start()
    for v in range(units):
        for near in range(2 * v, min(2 * v + 2, units)):
            for j in range(2):
                z_copy(1, near, j, grp).start()
        for d in range(2, n_grp):
            for j in range(2):
                z_copy(d, v, j, grp).start()
    own_x.start()
    x_copy().start()

    lane = lax.broadcasted_iota(jnp.int32, (rows, points), 1)
    eye = lax.broadcasted_iota(jnp.int32, (rows, points), 0) == lane
    steps = (1, 2, 4, 8, 16)

    def turn(values, amount):
        return pltpu.roll(values, amount % points, 1)

    def weights_of(at, code):
        shift_lanes = code[rows:rows + 8].astype(jnp.int32)[2:3].astype(jnp.float32)
        diagonal = jnp.where(eye, shift_lanes, 0.0).astype(jnp.bfloat16)
        shift = jnp.dot(
            diagonal, jnp.ones((points, points), jnp.bfloat16), preferred_element_type=jnp.float32
        ).astype(jnp.int32)
        bits = shift + 8
        for m, weight in enumerate(lagrange(decoded(code[0:rows].astype(jnp.int32)))):
            weight = weight.astype(jnp.bfloat16).astype(jnp.float32)
            for step in steps:
                weight = jnp.where((bits & step) != 0, turn(weight, step), weight)
            weight = turn(weight, m - 9)
            raw = lane - shift - (m - 1)
            inside = (raw >= 0) & (raw < points)
            wl[at, m] = jnp.where(inside, weight, 0.0)
            wl[at, 4 + m] = jnp.where(inside, 0.0, weight)
        wl[at, 8] = bits.astype(jnp.float32)

    wide = lax.broadcasted_iota(jnp.int32, (8, 2 * rows), 1)
    slot = lax.broadcasted_iota(jnp.int32, (tile_rows, 2 * rows), 0)

    def meta_of(at):
        return fr[at, rows:rows + 8].astype(jnp.int32).astype(jnp.float32)

    def table_of(at):
        both = jnp.where(wide < rows, meta_of(at), pltpu.roll(meta_of(at + 1), rows, 1))
        band = both[0:1].astype(jnp.int32)
        place = both[1:2].astype(jnp.int32)
        lat_weight = [w.astype(jnp.bfloat16).astype(jnp.float32) for w in lagrange(decoded(both[3:4]))]
        for j in range(2):
            for e, to in enumerate((chip, first[j], second[j], opposite)):
                far = slot - jnp.where(band == to * 2 + parity[j], place, -(1 << 20))
                table = jnp.zeros(far.shape, jnp.float32)
                for k in range(4):
                    table = jnp.where(far == k, lat_weight[k], table)
                am[pl.ds((j * n_chip + e) * tile_rows, tile_rows), pl.ds(at * rows, 2 * rows)] = table.astype(jnp.bfloat16)

    fr[grp] = fs[...]
    weights_of(grp, fs[...])
    for d in range(1, n_grp):
        f_copy(d, source(d)).wait_recv()
        n_copy(d).start()
        weights_of(source(d), fr[source(d)])
    for g in range(0, n_grp, 2):
        table_of(g)
    for d in range(n_grp):
        g = source(d)
        n_copy(d).wait_recv()
        weights_of(n_grp + g, fr[n_grp + g])
    for g in range(0, n_grp, 2):
        table_of(n_grp + g)
    own_x.wait()
    x_copy().wait_recv()

    def lon(at, v):
        bits = wl[at, 8].astype(jnp.int32)
        moved = xs[at, v].astype(jnp.float32)
        for step in steps:
            moved = jnp.where((bits & step) != 0, turn(moved, step), moved)
        own, spill = 0.0, 0.0
        for m in range(4):
            x = turn(moved, m - 9)
            own = own + x * wl[at, m]
            spill = spill + x * wl[at, 4 + m]
        place = pl.ds(at * rows, rows)
        rb[v % 2, place, 0:points] = own.astype(jnp.bfloat16)
        rb[v % 2, place, points:2 * points] = spill.astype(jnp.bfloat16)

    low = lax.broadcasted_iota(jnp.int32, (tile_rows, points), 1) < points // 2

    def arrive(v):
        for d in range(n_grp):
            for j in range(2):
                if d:
                    z_copy(d, v, j, source(d)).wait_recv()
            for j in range(2):
                lon(j * n_grp + source(d), v)

    def depart(v):
        whole = jnp.dot(am[...], rb[v % 2], preferred_element_type=jnp.float32)
        for j in range(2):
            for e in (3, 1, 2, 0):
                at = (j * n_chip + e) * tile_rows
                both = whole[at:at + tile_rows]
                own, spill = both[:, :points], both[:, points:]
                ahead = jnp.concatenate([spill[-TL:], spill[:-TL]], axis=0)
                behind = jnp.concatenate([spill[TL:], spill[:TL]], axis=0)
                total = own + jnp.where(low, ahead, behind)
                if e == 3:
                    s1[v, j, 1] = total.astype(jnp.bfloat16)
                    p_copy(v, j).start()
                elif e == 1:
                    s1[v, j, 0] = total.astype(jnp.bfloat16)
                    d_copy(v, j).start()
                elif e == 2:
                    pb[v % 2, j] = total
                elif j == 0:
                    out_ref[core * units + v] = total
                else:
                    s3[v] = total
                    o_copy(v).start()

    def middle(v):
        for j in range(2):
            p_copy(v, j).wait_recv()
            s2[v, j] = (pb[v % 2, j] + r1[v, j].astype(jnp.float32)).astype(jnp.bfloat16)
            e_copy(v, j).start()

    def finish(v):
        for j in range(2):
            d_copy(v, j).wait_recv()
            e_copy(v, j).wait_recv()
            at = parity[j] * units + v
            if j:
                o_copy(v).wait_recv()
            mine = r3[v] if j else out_ref[at]
            out_ref[at] = mine + q1[v, j].astype(jnp.float32) + q2[v, j].astype(jnp.float32)

    def chunk(v, carry):
        @pl.when(v < units)
        def _():
            arrive(v)
            depart(v)

        @pl.when((v >= 1) & (v < units + 1))
        def _():
            middle(v - 1)

        @pl.when(v >= 2)
        def _():
            finish(v - 2)

        return carry

    lax.fori_loop(0, units + 2, chunk, 0)

    n_copy(0).wait_send()
    x_copy().wait_send()
    for d in range(1, n_grp):
        f_copy(d, grp).wait_send()
        n_copy(d).wait_send()
    for v in range(units):
        o_copy(v).wait_send()
        for j in range(2):
            for d in range(1, n_grp):
                z_copy(d, v, j, grp).wait_send()
            d_copy(v, j).wait_send()
            p_copy(v, j).wait_send()
            e_copy(v, j).wait_send()


def fused(increments, band, tile_index, lat_offset, lon_shift, lat_frac, lon_frac):
    rows, fields, all_levels, points = increments.shape
    n_lat, n_grp = lax.axis_size("lat"), lax.axis_size("grp")
    n_chip = n_lat // 2
    levels = all_levels // n_grp
    tile_rows = TILES_DEV * TL
    units = levels * fields // 2
    x = jnp.transpose(increments, (2, 1, 0, 3)).reshape(all_levels * fields, rows, points)
    small = [a.reshape(1, rows) for a in (band, tile_index, lat_offset, lon_shift, lat_frac)]
    bf16, f32 = jnp.bfloat16, jnp.float32
    dma = pltpu.SemaphoreType.DMA
    sums = (units, 2, tile_rows, points)
    return pl.pallas_call(
        functools.partial(fused_kernel, n_lat, n_grp),
        out_shape=jax.ShapeDtypeStruct((2 * units, tile_rows, points), f32),
        in_specs=[pl.BlockSpec(memory_space=pltpu.VMEM)] * 7,
        out_specs=pl.BlockSpec(memory_space=pltpu.VMEM),
        scratch_shapes=[
            pltpu.VMEM((8, points), f32),
            pltpu.VMEM((rows + 8, points), jnp.int16),
            pltpu.VMEM((2 * n_grp, units, rows, points), bf16),
            pltpu.VMEM((2 * n_grp, rows + 8, points), jnp.int16),
            pltpu.VMEM((2 * n_grp, 9, rows, points), f32),
            pltpu.VMEM((n_lat * tile_rows, n_grp * 2 * rows), bf16),
            pltpu.VMEM((2, n_grp * 2 * rows, 2 * points), bf16),
            pltpu.VMEM((2, 2, tile_rows, points), f32),
            pltpu.VMEM((units, 2, 2, tile_rows, points), bf16),
            pltpu.VMEM(sums, bf16),
            pltpu.VMEM(sums, bf16),
            pltpu.VMEM(sums, bf16),
            pltpu.VMEM(sums, bf16),
            pltpu.VMEM((units, tile_rows, points), f32),
            pltpu.VMEM((units, tile_rows, points), f32),
            dma((n_grp, 2, units)),
            dma((n_grp, 2, units)),
            dma((n_grp,)),
            dma((n_grp,)),
            dma((n_grp,)),
            dma((n_grp,)),
            dma,
            dma,
            dma((units, 2)),
            dma((units, 2)),
            dma((units, 2)),
            dma((units, 2)),
            dma((units, 2)),
            dma((units, 2)),
            dma((units,)),
            dma((units,)),
            dma,
        ],
        compiler_params=pltpu.CompilerParams(
            collective_id=0, has_side_effects=True, vmem_limit_bytes=40 * 1024 * 1024
        ),
    )(x, lon_frac, *small).reshape(levels, fields, tile_rows, points)


def solution(mesh):
    in_specs = (
        P(("lat", "grp"), None, None, None),
        P(("lat", "grp"), None),
        P(("lat", "grp")),
        P(("lat", "grp")),
        P(("lat", "grp")),
        P(("lat", "grp")),
        P(("lat", "grp"), None),
    )
    out_specs = P("grp", None, "lat", None)
    n_lat, n_grp = mesh.shape["lat"], mesh.shape["grp"]

    def local(increments, *rest):
        rows = increments.shape[0]
        dense_rows = n_lat // 2 * TILES_DEV * TL
        slot_rows = n_grp * n_lat * (3 * rows // n_lat)
        grid = n_lat == 8 and n_grp > 1 and n_grp & (n_grp - 1) == 0
        step = fused if grid and dense_rows <= slot_rows else by_slots
        return step(increments, *rest)

    return jax.shard_map(local, mesh=mesh, in_specs=in_specs, out_specs=out_specs, check_vma=False)
```

time: 50.2 us -> 49.4 us (0.984)
  other arithmetic: 0.77 us -> 0 us
    convert_element_type x1 -> x0, other arithmetic: 0.77 us -> none  [fused(): coded = (jnp.round(lon_frac * 65535.0) - 32768.0).astype(jnp.int16)]
    unnamed x11 -> x13, local copies, waits for them, and re-layouts: 1.63 us -> 1.62 us
where the time goes in v1:
time: 49.4 us; the launch traced here: 49 us
  Pallas kernels  45.4 us (92%)
  local copies, waits for them, and re-layouts  3.53 us (7%)
    pallas_call x1, Pallas kernels, fused(): pl.pallas_call(functools.partial(fused_kernel, n_lat, n_grp), out_shape=j...  45.4 us
    transpose x1, local copies, waits for them, and re-layouts, fused(): jnp.transpose(increments, (2, 1, 0, 3))  1.91 us
    unnamed x13, local copies, waits for them, and re-layouts  1.62 us

profile of v1, /device:TPU:0, one launch (start us, length us, event | category | flops | bytes accessed | tf_op | source)
XLA Modules:
  0.0 49.0 jit_solution(445268290400827280)
XLA Ops:
  0.0 0.0 copy-start
  0.0 0.0 copy-start.4
  0.0 0.0 copy-start.5
  0.0 1.9 %copy.8 = bf16[16,4,64,128]{3,2,1,0:T(8,128)(2,1)S(1)} copy(bf16[16,4,64,128]{3,0,1,2:T(8,128)(2,1)} %bitcast.15) | data formatting | bytes 2097152 | tf_op jit(solution)/shard_map/transpose | solution.py:399
  1.9 0.0 copy-start.1
  1.9 0.0 copy-start.2
  1.9 0.0 copy-start.3
  2.0 0.0 copy-done
  2.0 0.0 copy-done.4
  2.0 0.0 copy-done.5
  2.0 0.6 %copy-done.1 = s32[64,1]{0,1:T(1,128)S(1)} copy-done((s32[64,1]{0,1:T(1,128)S(1)}, s32[64,1]{0,1:T(1,128)}, u32[]{:S(2)}) %copy-start.1) | copy-done | bytes 280
  2.6 0.0 copy-done.2
  2.6 0.0 copy-done.3
  2.6 45.4 %shard_map.73 = f32[16,128,128]{2,1,0:T(8,128)S(1)} custom-call(bf16[64,64,128]{2,1,0:T(8,128)(2,1)S(1)} %bitcast.9, f32[64,128]{1,0:T(8,128)S(1)} %copy-done, s32[1,64]{1,0:T(1,128)S(1)} %bitcast.10, s32[1,64]{1,0:T(1,128)S(1)} %bitcast.11, s32[1,64]{1,0:T(1,128)S(1)} %bitcast.12, s32[1,64]{1,0:T(1,128)S(1)} %bitcast.13, f32[1,64]{1,0:T(1,128)S(1)} %bitcast.14), custom_call_target="tpu_custom_call" | custom-call | tf_op jit(solution)/shard_map/pallas_call | solution.py:404
  48.0 1.0 %copy.10 = f32[4,4,128,128]{3,2,1,0:T(8,128)} copy(f32[4,4,128,128]{3,2,1,0:T(8,128)S(1)} %bitcast.8) | data formatting | bytes 2097152
Async XLA Ops:
  0.0 2.0 %copy-start = (f32[64,128]{1,0:T(8,128)S(1)}, f32[64,128]{1,0:T(8,128)}, u32[]{:S(2)}) copy-start(f32[64,128]{1,0:T(8,128)} %frac_ref.1) | copy-start | bytes 98308
  0.0 2.0 %copy-start.4 = (s32[64]{0:T(128)S(1)}, s32[64]{0:T(128)}, u32[]{:S(2)}) copy-start(s32[64]{0:T(128)} %param.11) | copy-start | bytes 772
  0.0 2.0 %copy-start.5 = (f32[64]{0:T(128)S(1)}, f32[64]{0:T(128)}, u32[]{:S(2)}) copy-start(f32[64]{0:T(128)} %param.12) | copy-start | bytes 772
  1.9 0.7 %copy-start.1 = (s32[64,1]{0,1:T(1,128)S(1)}, s32[64,1]{0,1:T(1,128)}, u32[]{:S(2)}) copy-start(s32[64,1]{0,1:T(1,128)} %param.8) | copy-start | bytes 772
  1.9 0.7 %copy-start.2 = (s32[64]{0:T(128)S(1)}, s32[64]{0:T(128)}, u32[]{:S(2)}) copy-start(s32[64]{0:T(128)} %param.9) | copy-start | bytes 772
  1.9 0.7 %copy-start.3 = (s32[64]{0:T(128)S(1)}, s32[64]{0:T(128)}, u32[]{:S(2)}) copy-start(s32[64]{0:T(128)} %param.10) | copy-start | bytes 772

commit v2 on v1

--- a/solution.py
+++ b/solution.py
@@ -130,12 +130,14 @@
 
 
 MESH = pl.DeviceIdType.MESH
-
-
-def fused_kernel(n_lat, n_grp, x_ref, frac_ref, band_ref, tile_ref, first_ref, shift_ref, part_ref, out_ref,
-                 meta_ref, fs, xs, fr, wl, am, rb, pb, s1, r1, q1, s2, q2, s3, r3,
+BLOCKS = ((0, 3), (1, 3), (0, 1), (1, 1), (1, 0), (0, 2), (1, 2), (0, 0))
+WINDOW = 2
+
+
+def fused_kernel(n_lat, n_grp, fields, x_hbm, frac_hbm, band_hbm, tile_hbm, first_hbm, shift_hbm, part_hbm, out_ref,
+                 frac_ref, band_ref, tile_ref, first_ref, shift_ref, part_ref, xn, xf, x_ref, meta_ref, fs, xs, fr, wl, am, rb, pb, s1, r1, q1, s2, q2, s3, r3,
                  z_send, z_recv, f_send, f_recv, n_send, n_recv, x_send, x_recv,
-                 d_send, d_recv, p_send, p_recv, e_send, e_recv, o_send, o_recv, loc_sem):
+                 d_send, d_recv, p_send, p_recv, e_send, e_recv, o_send, o_recv, loc_sem, in_sem, small_sem):
     lat = lax.axis_index("lat")
     grp = lax.axis_index("grp")
     chip, core = lat // 2, lat % 2
@@ -151,6 +153,17 @@
     across = (toggled(1), toggled(2))
     opposite = toggled(1) + toggled(2) - chip
     parity = (core, other)
+    small = [pltpu.make_async_copy(src, dst, small_sem.at[n]) for n, (src, dst) in enumerate(
+        ((frac_hbm, frac_ref), (band_hbm, band_ref), (tile_hbm, tile_ref), (first_hbm, first_ref),
+         (shift_hbm, shift_ref), (part_hbm, part_ref)))]
+    for copy in small:
+        copy.start()
+    pieces = in_sem.shape[0]
+    stretch = xn.shape[0] // pieces
+    loads = [pltpu.make_async_copy(x_hbm.at[pl.ds(n * stretch, stretch)], xn.at[pl.ds(n * stretch, stretch)], in_sem.at[n])
+             for n in range(pieces)]
+    for copy in loads:
+        copy.start()
     first = tuple(across[0] * (1 - q) + across[1] * q for q in parity)
     second = tuple(across[1] * (1 - q) + across[0] * q for q in parity)
 
@@ -173,6 +186,8 @@
     def decoded(code):
         return (code.astype(jnp.float32) + 32768.0) * (1.0 / 65535.0)
 
+    for copy in small:
+        copy.wait()
     meta_ref[...] = jnp.zeros_like(meta_ref)
     meta_ref[0:1, 0:rows] = band_ref[...].astype(jnp.float32)
     meta_ref[1:2, 0:rows] = (tile_ref[...] * TL + first_ref[...]).astype(jnp.float32)
@@ -181,6 +196,17 @@
     fs[0:rows] = coded(frac_ref[...]).astype(jnp.int32).astype(jnp.int16)
     fs[rows:rows + 8] = meta_ref[...].astype(jnp.int32).astype(jnp.int16)
 
+    levels = xn.shape[0] // (rows * fields)
+    stride = xf.shape[1] // rows
+    for n in range(pieces):
+        loads[n].wait()
+        for r in range(n * rows // pieces, (n + 1) * rows // pieces):
+            for f in range(fields):
+                xf[f, r * stride:r * stride + levels] = xn[pl.ds((r * fields + f) * levels, levels)].astype(jnp.float32)
+    for l in range(levels):
+        for f in range(fields):
+            x_ref[l * fields + f] = xf[f, pl.ds(l, rows, stride=stride)].astype(jnp.bfloat16)
+
     pl.semaphore_wait(barrier, 2 * (n_grp - 1) + 1 + 4)
 
     def remote(src, dst, send, recv, to):
@@ -221,6 +247,11 @@
     for d in range(1, n_grp):
         f_copy(n_grp - d, grp).start()
     n_copy(0).start()
+    def issue(v):
+        for d in range(n_grp - 1, 0, -1):
+            for j in range(2):
+                z_copy(d, v, j, grp).start()
+
     for v in range(units):
         for near in range(2 * v, min(2 * v + 2, units)):
             for j in range(2):
@@ -273,7 +304,7 @@
                 table = jnp.zeros(far.shape, jnp.float32)
                 for k in range(4):
                     table = jnp.where(far == k, lat_weight[k], table)
-                am[pl.ds((j * n_chip + e) * tile_rows, tile_rows), pl.ds(at * rows, 2 * rows)] = table.astype(jnp.bfloat16)
+                am[pl.ds(BLOCKS.index((j, e)) * tile_rows, tile_rows), pl.ds(at * rows, 2 * rows)] = table.astype(jnp.bfloat16)
 
     fr[grp] = fs[...]
     weights_of(grp, fs[...])
@@ -317,11 +348,11 @@
                 lon(j * n_grp + source(d), v)
 
     def depart(v):
-        whole = jnp.dot(am[...], rb[v % 2], preferred_element_type=jnp.float32)
-        for j in range(2):
-            for e in (3, 1, 2, 0):
-                at = (j * n_chip + e) * tile_rows
-                both = whole[at:at + tile_rows]
+        for part in range(1):
+            count = len(BLOCKS) * tile_rows
+            whole = jnp.dot(am[pl.ds(part * count, count)], rb[v % 2], preferred_element_type=jnp.float32)
+            for at, (j, e) in enumerate(BLOCKS):
+                both = whole[at * tile_rows:(at + 1) * tile_rows]
                 own, spill = both[:, :points], both[:, points:]
                 ahead = jnp.concatenate([spill[-TL:], spill[:-TL]], axis=0)
                 behind = jnp.concatenate([spill[TL:], spill[:TL]], axis=0)
@@ -360,6 +391,7 @@
         @pl.when(v < units)
         def _():
             arrive(v)
+
             depart(v)
 
         @pl.when((v >= 1) & (v < units + 1))
@@ -396,17 +428,22 @@
     levels = all_levels // n_grp
     tile_rows = TILES_DEV * TL
     units = levels * fields // 2
-    x = jnp.transpose(increments, (2, 1, 0, 3)).reshape(all_levels * fields, rows, points)
+    x = increments.reshape(rows * fields * all_levels, points)
     small = [a.reshape(1, rows) for a in (band, tile_index, lat_offset, lon_shift, lat_frac)]
     bf16, f32 = jnp.bfloat16, jnp.float32
     dma = pltpu.SemaphoreType.DMA
     sums = (units, 2, tile_rows, points)
     return pl.pallas_call(
-        functools.partial(fused_kernel, n_lat, n_grp),
+        functools.partial(fused_kernel, n_lat, n_grp, fields),
         out_shape=jax.ShapeDtypeStruct((2 * units, tile_rows, points), f32),
-        in_specs=[pl.BlockSpec(memory_space=pltpu.VMEM)] * 7,
+        in_specs=[pl.BlockSpec(memory_space=pltpu.HBM)] * 7,
         out_specs=pl.BlockSpec(memory_space=pltpu.VMEM),
         scratch_shapes=[
+            pltpu.VMEM((rows, points), f32),
+            *[pltpu.VMEM((1, rows), a.dtype) for a in small],
+            pltpu.VMEM((rows * fields * all_levels, points), bf16),
+            pltpu.VMEM((fields, rows * (all_levels + 8), points), f32),
+            pltpu.VMEM((all_levels * fields, rows, points), bf16),
             pltpu.VMEM((8, points), f32),
             pltpu.VMEM((rows + 8, points), jnp.int16),
             pltpu.VMEM((2 * n_grp, units, rows, points), bf16),
@@ -439,9 +476,11 @@
             dma((units,)),
             dma((units,)),
             dma,
+            dma((4,)),
+            dma((6,)),
         ],
         compiler_params=pltpu.CompilerParams(
-            collective_id=0, has_side_effects=True, vmem_limit_bytes=40 * 1024 * 1024
+            collective_id=0, has_side_effects=True, vmem_limit_bytes=54525952
         ),
     )(x, lon_frac, *small).reshape(levels, fields, tile_rows, points)
 

time: 49.4 us -> 48 us (0.972)
  local copies, waits for them, and re-layouts: 3.53 us -> 2.44 us
    transpose x1 -> x0, local copies, waits for them, and re-layouts: 1.91 us -> none  [fused(): jnp.transpose(increments, (2, 1, 0, 3))]
    unnamed x13, local copies, waits for them, and re-layouts: 1.62 us -> 2.44 us
where the time goes in v2:
time: 48 us; the launch traced here: 47.8 us
  Pallas kernels  45.3 us (94%)
  local copies, waits for them, and re-layouts  2.44 us (5%)
    pallas_call x1, Pallas kernels, fused(): pl.pallas_call(functools.partial(fused_kernel, n_lat, n_grp, fields), out...  45.3 us
    unnamed x13, local copies, waits for them, and re-layouts  2.44 us

profile of v2, /device:TPU:0, one launch (start us, length us, event | category | flops | bytes accessed | tf_op | source)
XLA Modules:
  0.0 47.8 jit_solution(11533431336021757789)
XLA Ops:
  0.0 0.0 copy-start.4
  0.0 0.0 copy-start.5
  0.0 0.0 copy-start.1
  0.0 0.0 copy-start.2
  0.0 0.0 copy-start.3
  0.0 0.6 %copy-done.4 = s32[64]{0:T(128)S(1)} copy-done((s32[64]{0:T(128)S(1)}, s32[64]{0:T(128)}, u32[]{:S(2)}) %copy-start.4) | copy-done | bytes 280
  0.7 0.0 copy-done.5
  0.7 0.0 copy-done.1
  0.7 0.0 copy-done.2
  0.7 0.0 copy-done.3
  0.7 0.0 copy-start
  0.7 0.8 %copy-done = f32[64,128]{1,0:T(8,128)S(1)} copy-done((f32[64,128]{1,0:T(8,128)S(1)}, f32[64,128]{1,0:T(8,128)}, u32[]{:S(2)}) %copy-start) | copy-done | bytes 32792
  1.5 45.3 %shard_map.73 = f32[16,128,128]{2,1,0:T(8,128)S(1)} custom-call(bf16[4096,128]{1,0:T(8,128)(2,1)} %bitcast.13, f32[64,128]{1,0:T(8,128)S(1)} %copy-done, s32[1,64]{1,0:T(1,128)S(1)} %bitcast.8, s32[1,64]{1,0:T(1,128)S(1)} %bitcast.9, s32[1,64]{1,0:T(1,128)S(1)} %bitcast.10, s32[1,64]{1,0:T(1,128)S(1)} %bitcast.11, f32[1,64]{1,0:T(1,128)S(1)} %bitcast.12), custom_call_target="tpu_custom_call" | custom-call | tf_op jit(solution)/shard_map/pallas_call | solution.py:436
  46.8 1.0 %copy.9 = f32[4,4,128,128]{3,2,1,0:T(8,128)} copy(f32[4,4,128,128]{3,2,1,0:T(8,128)S(1)} %bitcast.7) | data formatting | bytes 2097152
Async XLA Ops:
  0.0 0.7 %copy-start.4 = (s32[64]{0:T(128)S(1)}, s32[64]{0:T(128)}, u32[]{:S(2)}) copy-start(s32[64]{0:T(128)} %param.11) | copy-start | bytes 772
  0.0 0.7 %copy-start.5 = (f32[64]{0:T(128)S(1)}, f32[64]{0:T(128)}, u32[]{:S(2)}) copy-start(f32[64]{0:T(128)} %param.12) | copy-start | bytes 772
  0.0 0.7 %copy-start.1 = (s32[64,1]{0,1:T(1,128)S(1)}, s32[64,1]{0,1:T(1,128)}, u32[]{:S(2)}) copy-start(s32[64,1]{0,1:T(1,128)} %param.8) | copy-start | bytes 772
  0.0 0.7 %copy-start.2 = (s32[64]{0:T(128)S(1)}, s32[64]{0:T(128)}, u32[]{:S(2)}) copy-start(s32[64]{0:T(128)} %param.9) | copy-start | bytes 772
  0.0 0.7 %copy-start.3 = (s32[64]{0:T(128)S(1)}, s32[64]{0:T(128)}, u32[]{:S(2)}) copy-start(s32[64]{0:T(128)} %param.10) | copy-start | bytes 772
  0.7 0.8 %copy-start = (f32[64,128]{1,0:T(8,128)S(1)}, f32[64,128]{1,0:T(8,128)}, u32[]{:S(2)}) copy-start(f32[64,128]{1,0:T(8,128)} %frac_hbm.1) | copy-start | bytes 98308

commit v3 on v2

--- a/solution.py
+++ b/solution.py
@@ -248,17 +248,12 @@
         f_copy(n_grp - d, grp).start()
     n_copy(0).start()
     def issue(v):
-        for d in range(n_grp - 1, 0, -1):
+        for d in range(1, n_grp):
             for j in range(2):
                 z_copy(d, v, j, grp).start()
 
-    for v in range(units):
-        for near in range(2 * v, min(2 * v + 2, units)):
-            for j in range(2):
-                z_copy(1, near, j, grp).start()
-        for d in range(2, n_grp):
-            for j in range(2):
-                z_copy(d, v, j, grp).start()
+    for v in range(4):
+        issue(v)
     own_x.start()
     x_copy().start()
 
@@ -364,7 +359,7 @@
                     s1[v, j, 0] = total.astype(jnp.bfloat16)
                     d_copy(v, j).start()
                 elif e == 2:
-                    pb[v % 2, j] = total
+                    pb[v % 4, j] = total
                 elif j == 0:
                     out_ref[core * units + v] = total
                 else:
@@ -374,7 +369,7 @@
     def middle(v):
         for j in range(2):
             p_copy(v, j).wait_recv()
-            s2[v, j] = (pb[v % 2, j] + r1[v, j].astype(jnp.float32)).astype(jnp.bfloat16)
+            s2[v, j] = (pb[v % 4, j] + r1[v, j].astype(jnp.float32)).astype(jnp.bfloat16)
             e_copy(v, j).start()
 
     def finish(v):
@@ -392,19 +387,25 @@
         def _():
             arrive(v)
 
+        @pl.when((v < units - 4))
+        def _():
+            issue(v + 4)
+
+        @pl.when(v < units)
+        def _():
             depart(v)
 
         @pl.when((v >= 1) & (v < units + 1))
         def _():
             middle(v - 1)
 
-        @pl.when(v >= 2)
+        @pl.when(v >= 3)
         def _():
-            finish(v - 2)
+            finish(v - 3)
 
         return carry
 
-    lax.fori_loop(0, units + 2, chunk, 0)
+    lax.fori_loop(0, units + 3, chunk, 0)
 
     n_copy(0).wait_send()
     x_copy().wait_send()
@@ -451,7 +452,7 @@
             pltpu.VMEM((2 * n_grp, 9, rows, points), f32),
             pltpu.VMEM((n_lat * tile_rows, n_grp * 2 * rows), bf16),
             pltpu.VMEM((2, n_grp * 2 * rows, 2 * points), bf16),
-            pltpu.VMEM((2, 2, tile_rows, points), f32),
+            pltpu.VMEM((4, 2, tile_rows, points), f32),
             pltpu.VMEM((units, 2, 2, tile_rows, points), bf16),
             pltpu.VMEM(sums, bf16),
             pltpu.VMEM(sums, bf16),

time: 48 us -> 45.5 us (0.948)
  Pallas kernels: 45.3 us -> 42.8 us
    pallas_call x1, Pallas kernels: 45.3 us -> 42.8 us  [fused(): pl.pallas_call(functools.partial(fused_kernel, n_lat, n_grp, fields), out...]
where the time goes in v3:
time: 45.5 us; the launch traced here: 45.3 us
  Pallas kernels  42.8 us (94%)
  local copies, waits for them, and re-layouts  2.44 us (5%)
    pallas_call x1, Pallas kernels, fused(): pl.pallas_call(functools.partial(fused_kernel, n_lat, n_grp, fields), out...  42.8 us
    unnamed x13, local copies, waits for them, and re-layouts  2.44 us

profile of v3, /device:TPU:0, one launch (start us, length us, event | category | flops | bytes accessed | tf_op | source)
XLA Modules:
  0.0 45.3 jit_solution(7277761153751078425)
XLA Ops:
  0.0 0.0 copy-start.4
  0.0 0.0 copy-start.5
  0.0 0.0 copy-start.1
  0.0 0.0 copy-start.2
  0.0 0.0 copy-start.3
  0.0 0.6 %copy-done.4 = s32[64]{0:T(128)S(1)} copy-done((s32[64]{0:T(128)S(1)}, s32[64]{0:T(128)}, u32[]{:S(2)}) %copy-start.4) | copy-done | bytes 280
  0.7 0.0 copy-done.5
  0.7 0.0 copy-done.1
  0.7 0.0 copy-done.2
  0.7 0.0 copy-done.3
  0.7 0.0 copy-start
  0.7 0.8 %copy-done = f32[64,128]{1,0:T(8,128)S(1)} copy-done((f32[64,128]{1,0:T(8,128)S(1)}, f32[64,128]{1,0:T(8,128)}, u32[]{:S(2)}) %copy-start) | copy-done | bytes 32792
  1.5 42.8 %shard_map.73 = f32[16,128,128]{2,1,0:T(8,128)S(1)} custom-call(bf16[4096,128]{1,0:T(8,128)(2,1)} %bitcast.13, f32[64,128]{1,0:T(8,128)S(1)} %copy-done, s32[1,64]{1,0:T(1,128)S(1)} %bitcast.8, s32[1,64]{1,0:T(1,128)S(1)} %bitcast.9, s32[1,64]{1,0:T(1,128)S(1)} %bitcast.10, s32[1,64]{1,0:T(1,128)S(1)} %bitcast.11, f32[1,64]{1,0:T(1,128)S(1)} %bitcast.12), custom_call_target="tpu_custom_call" | custom-call | tf_op jit(solution)/shard_map/pallas_call | solution.py:437
  44.3 1.0 %copy.9 = f32[4,4,128,128]{3,2,1,0:T(8,128)} copy(f32[4,4,128,128]{3,2,1,0:T(8,128)S(1)} %bitcast.7) | data formatting | bytes 2097152
Async XLA Ops:
  0.0 0.7 %copy-start.4 = (s32[64]{0:T(128)S(1)}, s32[64]{0:T(128)}, u32[]{:S(2)}) copy-start(s32[64]{0:T(128)} %param.11) | copy-start | bytes 772
  0.0 0.7 %copy-start.5 = (f32[64]{0:T(128)S(1)}, f32[64]{0:T(128)}, u32[]{:S(2)}) copy-start(f32[64]{0:T(128)} %param.12) | copy-start | bytes 772
  0.0 0.7 %copy-start.1 = (s32[64,1]{0,1:T(1,128)S(1)}, s32[64,1]{0,1:T(1,128)}, u32[]{:S(2)}) copy-start(s32[64,1]{0,1:T(1,128)} %param.8) | copy-start | bytes 772
  0.0 0.7 %copy-start.2 = (s32[64]{0:T(128)S(1)}, s32[64]{0:T(128)}, u32[]{:S(2)}) copy-start(s32[64]{0:T(128)} %param.9) | copy-start | bytes 772
  0.0 0.7 %copy-start.3 = (s32[64]{0:T(128)S(1)}, s32[64]{0:T(128)}, u32[]{:S(2)}) copy-start(s32[64]{0:T(128)} %param.10) | copy-start | bytes 772
  0.7 0.8 %copy-start = (f32[64,128]{1,0:T(8,128)S(1)}, f32[64,128]{1,0:T(8,128)}, u32[]{:S(2)}) copy-start(f32[64,128]{1,0:T(8,128)} %frac_hbm.1) | copy-start | bytes 98308
